TPU v7x, 32 devices: a whole 2x2x4 slice. The times are simulated.
32 devices in a mesh: grp: 2 (over core), row: 2 (over y), col: 8 (over z, x).
Axes of the slice: x: 2, y: 2, z: 4, core: 2. Of those that a mesh axis runs over, the one named last changes fastest.
Arguments:
- load: float32 [4, 8, 1024, 256], P(('grp', 'row'), 'col'), may hold values from -6 to 6
- guess: float32 [4, 8, 1024, 256], P(('grp', 'row'), 'col'), may hold values from -6 to 6
- interface_op: bfloat16 [4, 8, 1024, 1024], P(('grp', 'row'), 'col'), may hold values from -1 to 5
- precond: bfloat16 [4, 8, 1024, 1024], P(('grp', 'row'), 'col'), may hold values from -1 to 2
- basis: bfloat16 [4, 8, 1024, 64], P(('grp', 'row'), 'col'), may hold values from -0.375 to 0.375
- coarse_inverse: bfloat16 [2048, 2048], P(('grp', 'row'), 'col'), may hold values from -0.1875 to 0.1875
- edge_rows: int32 [4, 8, 1024], P(('grp', 'row'), 'col'), may hold values from 0 to 1023, each once within a row
- coarse_slot: int32 [4, 8, 64], P(('grp', 'row'), 'col'), may hold values from 0 to 63, each once within a row
Outputs:
- displacement: float32 [4, 8, 1024, 256], P(('grp', 'row'), 'col')
Inputs may be any that keep to these rules, and one draw needn't show every extreme that they name: `edge_rows`: each subdomain lists each of its 1024 interface rows once. `coarse_slot`: each subdomain gives each of its 64 basis vectors a different offset.
All inputs are finite; a program needn't handle non-finite values.
Results may differ from a plain program's by a relative error of at most 0.0095.
Values may be sent and summed in bfloat16 or wider, within the bound.
No kernel may reach another device: no remote copies, remote signals or barrier semaphores. Data moves between devices by JAX's collectives and lax.ppermute only.
A program may use at most 64 MiB of HBM per device.

v0:
```python
import jax
import jax.numpy as jnp
from jax import lax
from jax.sharding import PartitionSpec as P

ITERS = 2
OMEGA = 0.6


def extended(shard, sides, width):
    for axis, dim in sides:
        size, length = (lax.axis_size(axis), shard.shape[dim])
        up = [(i, (i + 1) % size) for i in range(size - 1)]
        down = [(j, i) for i, j in up]
        last = lax.slice_in_dim(shard, length - width, length, axis=dim)
        first = lax.slice_in_dim(shard, 0, width, axis=dim)
        before = lax.ppermute(last, axis, up)
        after = lax.ppermute(first, axis, down)
        shard = jnp.concatenate([before, shard, after], axis=dim)
    return shard


def body(load, guess, interface_op, precond, basis, coarse_inverse, edge_rows, coarse_slot):
    local_load = load[0, 0]
    current = guess[0, 0]
    operator_block = interface_op[0, 0]
    precond_block = precond[0, 0]
    basis_block = basis[0, 0]
    row_order = edge_rows[0, 0]
    slot_order = coarse_slot[0, 0]
    n_unknowns, n_cases = local_load.shape
    edge_len = n_unknowns // 4
    n_basis = basis_block.shape[1]
    block_len = coarse_inverse.shape[1]
    grid_rows = lax.axis_size(("grp", "row"))
    grid_cols = lax.axis_size("col")
    my_row = lax.axis_index(("grp", "row"))
    my_col = lax.axis_index("col")
    present = jnp.stack([my_col > 0, my_col < grid_cols - 1, my_row > 0, my_row < grid_rows - 1])
    present = present.astype(jnp.float32)[:, None, None]
    selector = (slot_order[:, None] == jnp.arange(n_basis, dtype=jnp.int32)[None, :]).astype(
        jnp.bfloat16
    )
    contract_first = (((0,), (0,)), ((), ()))

    def place(values):
        blank = jnp.zeros((n_unknowns, n_cases), jnp.float32)
        return blank.at[row_order].set(values.reshape(n_unknowns, n_cases))

    def traces(values):
        own = values[row_order].reshape(4, edge_len, n_cases)
        across_cols = extended(own[0:2], (("col", 0),), 1)
        across_rows = extended(own[2:4], ((("grp", "row"), 0),), 1)
        beside = jnp.stack([across_cols[0], across_cols[3], across_rows[0], across_rows[3]])
        return (own, beside)

    for sweep in range(ITERS):
        applied = jnp.dot(
            operator_block, current.astype(jnp.bfloat16), preferred_element_type=jnp.float32
        )
        own_applied, beside_applied = traces(applied)
        resid = local_load - applied - place(beside_applied)
        resid_bf = resid.astype(jnp.bfloat16)
        local_fix = jnp.dot(precond_block, resid_bf, preferred_element_type=jnp.float32)
        fine_own, fine_beside = traces(local_fix)
        smooth_fix = local_fix + 0.5 * place(present * (fine_beside - fine_own))
        coarse_res = lax.dot_general(
            basis_block, resid_bf, contract_first, preferred_element_type=jnp.float32
        ).astype(jnp.bfloat16)
        ordered = lax.dot_general(
            selector, coarse_res, contract_first, preferred_element_type=jnp.float32
        ).astype(jnp.bfloat16)
        row_block = lax.all_gather(ordered, "col", axis=0, tiled=True)
        source = lax.all_gather(row_block, ("grp", "row"), axis=0, tiled=True)
        offset = my_col * block_len
        column_part = lax.dynamic_slice_in_dim(source, offset, block_len, 0)
        summed = lax.psum_scatter(
            jnp.dot(coarse_inverse, column_part, preferred_element_type=jnp.float32),
            "col",
            scatter_dimension=0,
            tiled=True,
        ).astype(jnp.bfloat16)
        picked = jnp.dot(selector, summed, preferred_element_type=jnp.float32).astype(jnp.bfloat16)
        coarse_fix = jnp.dot(basis_block, picked, preferred_element_type=jnp.float32)
        current = current + OMEGA * (smooth_fix + coarse_fix)
    return current[None, None]


def solution(mesh):
    return jax.shard_map(
        body,
        mesh=mesh,
        in_specs=(
            P(("grp", "row"), "col", None, None),
            P(("grp", "row"), "col", None, None),
            P(("grp", "row"), "col", None, None),
            P(("grp", "row"), "col", None, None),
            P(("grp", "row"), "col", None, None),
            P(("grp", "row"), "col"),
            P(("grp", "row"), "col", None),
            P(("grp", "row"), "col", None),
        ),
        out_specs=P(("grp", "row"), "col", None, None),
        check_vma=False,
    )
```

profile of v0, /device:TPU:0, one launch (start us, length us, event | category | flops | bytes accessed | tf_op | source)
XLA Modules:
  0.0 328.5 jit_solution(16232925203345687816)
XLA Ops:
  8.1 1.9 fusion.6
  10.1 4.7 %gather_fusion = f32[1024,256]{1,0:T(8,128)} fusion(f32[1024,256]{1,0:T(8,128)S(1)} %fusion.6, s32[1024]{0:T(1024)S(1)} %broadcast_clamp_fusion), kind=kCustom, calls=%fused_computation | custom fusion | bytes 2101248 | tf_op jit(solution)/shard_map/gather | solution.py:51
  14.8 1.3 slice_bitcast_fusion.15
  16.0 4.9 %collective-permute-start = (f32[1,256,256]{2,1,0:T(8,128)S(1)}, f32[1,256,256]{2,1,0:T(8,128)S(1)}, u32[]{:S(2)}, u32[]{:S(2)}) collective-permute-start(f32[1,256,256]{2,1,0:T(8,128)S(1)} %get-tuple-element.17), channel_id=1, source_target_pairs={{0,1},{1,2},{2,3},{3,4},{4,5},{5,6},{6,7},{8,9},{9,10},{10,11},{11... | collective-permute-start | bytes 786440 | tf_op jit(solution)/shard_map/ppermute | solution.py:17
  20.9 3.4 %collective-permute-start.2 = (f32[1,256,256]{2,1,0:T(8,128)S(1)}, f32[1,256,256]{2,1,0:T(8,128)S(1)}, u32[]{:S(2)}, u32[]{:S(2)}) collective-permute-start(f32[1,256,256]{2,1,0:T(8,128)S(1)} %get-tuple-element.18), channel_id=1, source_target_pairs={{0,8},{8,16},{16,24},{1,9},{9,17},{17,25},{2,10},{10,18},{18,26},{... | collective-permute-start | bytes 786440 | tf_op jit(solution)/shard_map/ppermute | solution.py:17
  24.4 1.3 collective-permute-start.1
  25.7 1.3 collective-permute-start.3
  27.0 4.0 %collective-permute-done.2 = f32[1,256,256]{2,1,0:T(8,128)S(1)} collective-permute-done((f32[1,256,256]{2,1,0:T(8,128)S(1)}, f32[1,256,256]{2,1,0:T(8,128)S(1)}, u32[]{:S(2)}, u32[]{:S(2)}) %collective-permute-start.2) | collective-permute-done | bytes 262176 | tf_op jit(solution)/shard_map/ppermute | solution.py:17
  31.0 2.7 collective-permute-done.1
  33.8 1.3 collective-permute-done.3
  35.1 1.0 pad_maximum_fusion
  36.1 6.3 %scatter_custom_fusion = f32[1024,256]{1,0:T(8,128)} fusion(s32[1024]{0:T(1024)S(1)} %bitcast.145, f32[1024,256]{1,0:T(8,128)} %bitcast.140, f32[]{:T(128)} %constant.14.clone.1), kind=kCustom, calls=%fused_computation.58 | custom fusion | bytes 1049088 | tf_op jit(solution)/shard_map/scatter | solution.py:48
  42.4 2.5 fusion.27
  44.9 1.4 convolution_convert_fusion.5
  46.3 34.9 %all_gather.12 = bf16[512,256]{1,0:T(8,128)(2,1)} all-gather(bf16[64,256]{1,0:T(8,128)(2,1)S(1)} %convolution_convert_fusion.5), channel_id=1, replica_groups=mesh['grp'=2,'row'=2,'col'=8] {'col'}, dimensions={0}, use_global_device_ids=true | all-gather | bytes 294912 | tf_op jit(solution)/shard_map/all_gather | solution.py:73
  81.2 15.8 %all-gather.3.cloned.1.call-done = bf16[2048,256]{1,0:T(8,128)(2,1)} async-done(((bf16[512,256]{1,0:T(8,128)(2,1)}), bf16[2048,256]{1,0:T(8,128)(2,1)}) %all-gather.3.cloned.1.call-update) | async-done | bytes 1048592 | tf_op jit(solution)/shard_map/all_gather | solution.py:74
  97.1 1.2 convolution_bitcast_fusion.3
  99.3 2.4 fusion.14
  101.7 4.7 %gather_fusion.1 = f32[1024,256]{1,0:T(8,128)} fusion(f32[1024,256]{1,0:T(8,128)S(1)} %fusion.14, s32[1024]{0:T(1024)S(1)} %broadcast_clamp_fusion), kind=kCustom, calls=%fused_computation.1 | custom fusion | bytes 2101248 | tf_op jit(solution)/shard_map/gather | solution.py:51
  106.4 1.4 slice_bitcast_fusion.11
  107.8 3.4 %collective-permute-start.4 = (f32[1,256,256]{2,1,0:T(8,128)S(1)}, f32[1,256,256]{2,1,0:T(8,128)S(1)}, u32[]{:S(2)}, u32[]{:S(2)}) collective-permute-start(f32[1,256,256]{2,1,0:T(8,128)S(1)} %get-tuple-element.13), channel_id=1, source_target_pairs={{0,1},{1,2},{2,3},{3,4},{4,5},{5,6},{6,7},{8,9},{9,10},{10,11},{11... | collective-permute-start | bytes 786440 | tf_op jit(solution)/shard_map/ppermute | solution.py:17
  111.2 1.3 collective-permute-start.7
  112.5 4.6 %collective-permute-start.6 = (f32[1,256,256]{2,1,0:T(8,128)S(1)}, f32[1,256,256]{2,1,0:T(8,128)S(1)}, u32[]{:S(2)}, u32[]{:S(2)}) collective-permute-start(f32[1,256,256]{2,1,0:T(8,128)S(1)} %get-tuple-element.15), channel_id=1, source_target_pairs={{0,8},{8,16},{16,24},{1,9},{9,17},{17,25},{2,10},{10,18},{18,26},{... | collective-permute-start | bytes 786440 | tf_op jit(solution)/shard_map/ppermute | solution.py:17
  117.0 1.3 collective-permute-start.5
  118.5 2.7 collective-permute-done.7
  121.2 1.3 collective-permute-done.6
  122.5 4.4 %collective-permute-done.5 = f32[1,256,256]{2,1,0:T(8,128)S(1)} collective-permute-done((f32[1,256,256]{2,1,0:T(8,128)S(1)}, f32[1,256,256]{2,1,0:T(8,128)S(1)}, u32[]{:S(2)}, u32[]{:S(2)}) %collective-permute-start.5) | collective-permute-done | bytes 262176 | tf_op jit(solution)/shard_map/ppermute | solution.py:18
  127.0 1.2 fusion.25
  128.2 6.3 %scatter_custom_fusion.1 = f32[1024,256]{1,0:T(8,128)} fusion(s32[1024]{0:T(1024)S(1)} %bitcast.146, f32[1024,256]{1,0:T(8,128)} %fusion.25, f32[]{:T(128)} %constant.14.clone.1), kind=kCustom, calls=%fused_computation.56 | custom fusion | bytes 1049088 | tf_op jit(solution)/shard_map/scatter | solution.py:48
  134.5 28.8 %reduce-scatter.7.cloned.1.call-done = f32[64,256]{1,0:T(8,128)} async-done(((f32[512,256]{1,0:T(8,128)}), f32[64,256]{1,0:T(8,128)}) %reduce-scatter.7.cloned.1.call-update) | async-done | bytes 65552
  163.2 1.6 copy.30
  164.8 3.0 fusion.21
  167.8 1.9 fusion.8
  169.8 4.7 %gather_fusion.2 = f32[1024,256]{1,0:T(8,128)} fusion(f32[1024,256]{1,0:T(8,128)S(1)} %fusion.8, s32[1024]{0:T(1024)S(1)} %broadcast_clamp_fusion), kind=kCustom, calls=%fused_computation.2 | custom fusion | bytes 2101248 | tf_op jit(solution)/shard_map/gather | solution.py:51
  174.4 1.3 slice_bitcast_fusion.7
  175.7 3.2 collective-permute-start.8
  178.9 3.4 %collective-permute-start.10 = (f32[1,256,256]{2,1,0:T(8,128)S(1)}, f32[1,256,256]{2,1,0:T(8,128)S(1)}, u32[]{:S(2)}, u32[]{:S(2)}) collective-permute-start(f32[1,256,256]{2,1,0:T(8,128)S(1)} %get-tuple-element.10), channel_id=1, source_target_pairs={{0,8},{8,16},{16,24},{1,9},{9,17},{17,25},{2,10},{10,18},{18,26},{... | collective-permute-start | bytes 786440 | tf_op jit(solution)/shard_map/ppermute | solution.py:17
  182.3 1.3 collective-permute-start.9
  183.6 1.5 collective-permute-start.11
  185.1 1.2 collective-permute-done.10
  186.3 4.3 %collective-permute-done.9 = f32[1,256,256]{2,1,0:T(8,128)S(1)} collective-permute-done((f32[1,256,256]{2,1,0:T(8,128)S(1)}, f32[1,256,256]{2,1,0:T(8,128)S(1)}, u32[]{:S(2)}, u32[]{:S(2)}) %collective-permute-start.9) | collective-permute-done | bytes 262176 | tf_op jit(solution)/shard_map/ppermute | solution.py:18
  190.6 1.7 collective-permute-done.11
  192.3 1.0 pad_maximum_fusion.2
  193.3 6.3 %scatter_custom_fusion.2 = f32[1024,256]{1,0:T(8,128)} fusion(s32[1024]{0:T(1024)S(1)} %bitcast.147, f32[1024,256]{1,0:T(8,128)} %bitcast.141, f32[]{:T(128)} %constant.14.clone.1), kind=kCustom, calls=%fused_computation.54 | custom fusion | bytes 1049088 | tf_op jit(solution)/shard_map/scatter | solution.py:48
  199.6 2.5 fusion.29
  202.1 1.4 convolution_convert_fusion.3
  203.4 33.6 %all_gather.14 = bf16[512,256]{1,0:T(8,128)(2,1)} all-gather(bf16[64,256]{1,0:T(8,128)(2,1)S(1)} %convolution_convert_fusion.3), channel_id=1, replica_groups=mesh['grp'=2,'row'=2,'col'=8] {'col'}, dimensions={0}, use_global_device_ids=true | all-gather | bytes 294912 | tf_op jit(solution)/shard_map/all_gather | solution.py:73
  237.2 14.9 %all-gather.5.cloned.1.call-done = bf16[2048,256]{1,0:T(8,128)(2,1)} async-done(((bf16[512,256]{1,0:T(8,128)(2,1)}), bf16[2048,256]{1,0:T(8,128)(2,1)}) %all-gather.5.cloned.1.call-update) | async-done | bytes 1048592 | tf_op jit(solution)/shard_map/all_gather | solution.py:74
  252.0 1.2 convolution_bitcast_fusion.2
  253.2 1.0 copy.31
  254.2 2.4 fusion.11
  256.6 4.7 %gather_fusion.3 = f32[1024,256]{1,0:T(8,128)} fusion(f32[1024,256]{1,0:T(8,128)S(1)} %fusion.11, s32[1024]{0:T(1024)S(1)} %broadcast_clamp_fusion), kind=kCustom, calls=%fused_computation.3 | custom fusion | bytes 2101248 | tf_op jit(solution)/shard_map/gather | solution.py:51
  261.3 1.4 slice_bitcast_fusion.3
  262.7 3.4 %collective-permute-start.12 = (f32[1,256,256]{2,1,0:T(8,128)S(1)}, f32[1,256,256]{2,1,0:T(8,128)S(1)}, u32[]{:S(2)}, u32[]{:S(2)}) collective-permute-start(f32[1,256,256]{2,1,0:T(8,128)S(1)} %get-tuple-element.5), channel_id=1, source_target_pairs={{0,1},{1,2},{2,3},{3,4},{4,5},{5,6},{6,7},{8,9},{9,10},{10,11},{11... | collective-permute-start | bytes 786440 | tf_op jit(solution)/shard_map/ppermute | solution.py:17
  266.1 1.3 collective-permute-start.15
  267.4 4.6 %collective-permute-start.14 = (f32[1,256,256]{2,1,0:T(8,128)S(1)}, f32[1,256,256]{2,1,0:T(8,128)S(1)}, u32[]{:S(2)}, u32[]{:S(2)}) collective-permute-start(f32[1,256,256]{2,1,0:T(8,128)S(1)} %get-tuple-element.7), channel_id=1, source_target_pairs={{0,8},{8,16},{16,24},{1,9},{9,17},{17,25},{2,10},{10,18},{18,26},{... | collective-permute-start | bytes 786440 | tf_op jit(solution)/shard_map/ppermute | solution.py:17
  271.9 1.3 collective-permute-start.13
  273.2 2.9 collective-permute-done.15
  276.1 1.3 collective-permute-done.14
  277.5 4.4 %collective-permute-done.13 = f32[1,256,256]{2,1,0:T(8,128)S(1)} collective-permute-done((f32[1,256,256]{2,1,0:T(8,128)S(1)}, f32[1,256,256]{2,1,0:T(8,128)S(1)}, u32[]{:S(2)}, u32[]{:S(2)}) %collective-permute-start.13) | collective-permute-done | bytes 262176 | tf_op jit(solution)/shard_map/ppermute | solution.py:18
  282.0 1.2 fusion.24
  283.1 6.3 %scatter_custom_fusion.3 = f32[1024,256]{1,0:T(8,128)} fusion(s32[1024]{0:T(1024)S(1)} %bitcast.148, f32[1024,256]{1,0:T(8,128)} %fusion.24, f32[]{:T(128)} %constant.14.clone.1), kind=kCustom, calls=%fused_computation.52 | custom fusion | bytes 1049088 | tf_op jit(solution)/shard_map/scatter | solution.py:48
  289.4 28.6 %reduce-scatter.9.cloned.1.call-done = f32[64,256]{1,0:T(8,128)} async-done(((f32[512,256]{1,0:T(8,128)}), f32[64,256]{1,0:T(8,128)}) %reduce-scatter.9.cloned.1.call-update) | async-done | bytes 65552
  319.0 3.0 fusion.23
  (33 shorter events, 4.1 us)
Async XLA Ops:
  6.5 1.6 copy-start
  6.5 90.5 %all-gather.3.cloned.1.call-start = ((), (), s32[]{:S(2)}) async-start(), calls=%async_computation.2 | async-start | bytes 1310720 | tf_op jit(solution)/shard_map/all_gather | solution.py:74
  16.0 10.9 %collective-permute-start = (f32[1,256,256]{2,1,0:T(8,128)S(1)}, f32[1,256,256]{2,1,0:T(8,128)S(1)}, u32[]{:S(2)}, u32[]{:S(2)}) collective-permute-start(f32[1,256,256]{2,1,0:T(8,128)S(1)} %get-tuple-element.17), channel_id=1, source_target_pairs={{0,1},{1,2},{2,3},{3,4},{4,5},{5,6},{6,7},{8,9},{9,10},{10,11},{11... | collective-permute-start | bytes 786440 | tf_op jit(solution)/shard_map/ppermute | solution.py:17
  20.9 10.1 %collective-permute-start.2 = (f32[1,256,256]{2,1,0:T(8,128)S(1)}, f32[1,256,256]{2,1,0:T(8,128)S(1)}, u32[]{:S(2)}, u32[]{:S(2)}) collective-permute-start(f32[1,256,256]{2,1,0:T(8,128)S(1)} %get-tuple-element.18), channel_id=1, source_target_pairs={{0,8},{8,16},{16,24},{1,9},{9,17},{17,25},{2,10},{10,18},{18,26},{... | collective-permute-start | bytes 786440 | tf_op jit(solution)/shard_map/ppermute | solution.py:17
  24.4 9.4 %collective-permute-start.1 = (f32[1,256,256]{2,1,0:T(8,128)S(1)}, f32[1,256,256]{2,1,0:T(8,128)S(1)}, u32[]{:S(2)}, u32[]{:S(2)}) collective-permute-start(f32[1,256,256]{2,1,0:T(8,128)S(1)} %get-tuple-element.19), channel_id=1, source_target_pairs={{1,0},{2,1},{3,2},{4,3},{5,4},{6,5},{7,6},{9,8},{10,9},{11,10},{12... | collective-permute-start | bytes 786440 | tf_op jit(solution)/shard_map/ppermute | solution.py:18
  25.7 9.4 %collective-permute-start.3 = (f32[1,256,256]{2,1,0:T(8,128)S(1)}, f32[1,256,256]{2,1,0:T(8,128)S(1)}, u32[]{:S(2)}, u32[]{:S(2)}) collective-permute-start(f32[1,256,256]{2,1,0:T(8,128)S(1)} %get-tuple-element.20), channel_id=1, source_target_pairs={{8,0},{16,8},{24,16},{9,1},{17,9},{25,17},{10,2},{18,10},{26,18},{... | collective-permute-start | bytes 786440 | tf_op jit(solution)/shard_map/ppermute | solution.py:18
  42.4 2.6 copy-start.3
  42.4 2.6 copy-start.5
  42.4 54.7 %copy-start.4 = (bf16[512,256]{1,0:T(8,128)(2,1)S(1)}, bf16[512,256]{1,0:T(8,128)(2,1)}, u32[]{:S(2)}) copy-start(bf16[512,256]{1,0:T(8,128)(2,1)} %param.13) | copy-start | bytes 786436
  81.2 82.1 %reduce-scatter.7.cloned.1.call-start = ((), (), s32[]{:S(2)}) async-start(), calls=%async_computation.4 | async-start | bytes 589824
  99.3 152.8 %all-gather.5.cloned.1.call-start = ((), (), s32[]{:S(2)}) async-start(), calls=%async_computation.3 | async-start | bytes 1310720 | tf_op jit(solution)/shard_map/all_gather | solution.py:74
  106.4 20.6 %copy-start.1 = (f32[1024,256]{1,0:T(8,128)S(1)}, f32[1024,256]{1,0:T(8,128)}, u32[]{:S(2)}) copy-start(f32[1024,256]{1,0:T(8,128)} %gather_fusion.1) | copy-start | bytes 3145732
  107.8 10.7 %collective-permute-start.4 = (f32[1,256,256]{2,1,0:T(8,128)S(1)}, f32[1,256,256]{2,1,0:T(8,128)S(1)}, u32[]{:S(2)}, u32[]{:S(2)}) collective-permute-start(f32[1,256,256]{2,1,0:T(8,128)S(1)} %get-tuple-element.13), channel_id=1, source_target_pairs={{0,1},{1,2},{2,3},{3,4},{4,5},{5,6},{6,7},{8,9},{9,10},{10,11},{11... | collective-permute-start | bytes 786440 | tf_op jit(solution)/shard_map/ppermute | solution.py:17
  111.2 10.0 %collective-permute-start.7 = (f32[1,256,256]{2,1,0:T(8,128)S(1)}, f32[1,256,256]{2,1,0:T(8,128)S(1)}, u32[]{:S(2)}, u32[]{:S(2)}) collective-permute-start(f32[1,256,256]{2,1,0:T(8,128)S(1)} %get-tuple-element.14), channel_id=1, source_target_pairs={{8,0},{16,8},{24,16},{9,1},{17,9},{25,17},{10,2},{18,10},{26,18},{... | collective-permute-start | bytes 786440 | tf_op jit(solution)/shard_map/ppermute | solution.py:18
  112.5 10.1 %collective-permute-start.6 = (f32[1,256,256]{2,1,0:T(8,128)S(1)}, f32[1,256,256]{2,1,0:T(8,128)S(1)}, u32[]{:S(2)}, u32[]{:S(2)}) collective-permute-start(f32[1,256,256]{2,1,0:T(8,128)S(1)} %get-tuple-element.15), channel_id=1, source_target_pairs={{0,8},{8,16},{16,24},{1,9},{9,17},{17,25},{2,10},{10,18},{18,26},{... | collective-permute-start | bytes 786440 | tf_op jit(solution)/shard_map/ppermute | solution.py:17
  117.0 9.9 %collective-permute-start.5 = (f32[1,256,256]{2,1,0:T(8,128)S(1)}, f32[1,256,256]{2,1,0:T(8,128)S(1)}, u32[]{:S(2)}, u32[]{:S(2)}) collective-permute-start(f32[1,256,256]{2,1,0:T(8,128)S(1)} %get-tuple-element.16), channel_id=1, source_target_pairs={{1,0},{2,1},{3,2},{4,3},{5,4},{6,5},{7,6},{9,8},{10,9},{11,10},{12... | collective-permute-start | bytes 786440 | tf_op jit(solution)/shard_map/ppermute | solution.py:18
  175.7 9.4 %collective-permute-start.8 = (f32[1,256,256]{2,1,0:T(8,128)S(1)}, f32[1,256,256]{2,1,0:T(8,128)S(1)}, u32[]{:S(2)}, u32[]{:S(2)}) collective-permute-start(f32[1,256,256]{2,1,0:T(8,128)S(1)} %get-tuple-element.9), channel_id=1, source_target_pairs={{0,1},{1,2},{2,3},{3,4},{4,5},{5,6},{6,7},{8,9},{9,10},{10,11},{11... | collective-permute-start | bytes 786440 | tf_op jit(solution)/shard_map/ppermute | solution.py:17
  178.9 7.4 %collective-permute-start.10 = (f32[1,256,256]{2,1,0:T(8,128)S(1)}, f32[1,256,256]{2,1,0:T(8,128)S(1)}, u32[]{:S(2)}, u32[]{:S(2)}) collective-permute-start(f32[1,256,256]{2,1,0:T(8,128)S(1)} %get-tuple-element.10), channel_id=1, source_target_pairs={{0,8},{8,16},{16,24},{1,9},{9,17},{17,25},{2,10},{10,18},{18,26},{... | collective-permute-start | bytes 786440 | tf_op jit(solution)/shard_map/ppermute | solution.py:17
  182.3 8.3 %collective-permute-start.9 = (f32[1,256,256]{2,1,0:T(8,128)S(1)}, f32[1,256,256]{2,1,0:T(8,128)S(1)}, u32[]{:S(2)}, u32[]{:S(2)}) collective-permute-start(f32[1,256,256]{2,1,0:T(8,128)S(1)} %get-tuple-element.11), channel_id=1, source_target_pairs={{1,0},{2,1},{3,2},{4,3},{5,4},{6,5},{7,6},{9,8},{10,9},{11,10},{12... | collective-permute-start | bytes 786440 | tf_op jit(solution)/shard_map/ppermute | solution.py:18
  183.6 8.6 %collective-permute-start.11 = (f32[1,256,256]{2,1,0:T(8,128)S(1)}, f32[1,256,256]{2,1,0:T(8,128)S(1)}, u32[]{:S(2)}, u32[]{:S(2)}) collective-permute-start(f32[1,256,256]{2,1,0:T(8,128)S(1)} %get-tuple-element.12), channel_id=1, source_target_pairs={{8,0},{16,8},{24,16},{9,1},{17,9},{25,17},{10,2},{18,10},{26,18},{... | collective-permute-start | bytes 786440 | tf_op jit(solution)/shard_map/ppermute | solution.py:18
  237.1 80.9 %reduce-scatter.9.cloned.1.call-start = ((), (), s32[]{:S(2)}) async-start(), calls=%async_computation.5 | async-start | bytes 589824
  261.3 20.6 %copy-start.2 = (f32[1024,256]{1,0:T(8,128)S(1)}, f32[1024,256]{1,0:T(8,128)}, u32[]{:S(2)}) copy-start(f32[1024,256]{1,0:T(8,128)} %gather_fusion.3) | copy-start | bytes 3145732
  262.7 10.5 %collective-permute-start.12 = (f32[1,256,256]{2,1,0:T(8,128)S(1)}, f32[1,256,256]{2,1,0:T(8,128)S(1)}, u32[]{:S(2)}, u32[]{:S(2)}) collective-permute-start(f32[1,256,256]{2,1,0:T(8,128)S(1)} %get-tuple-element.5), channel_id=1, source_target_pairs={{0,1},{1,2},{2,3},{3,4},{4,5},{5,6},{6,7},{8,9},{9,10},{10,11},{11... | collective-permute-start | bytes 786440 | tf_op jit(solution)/shard_map/ppermute | solution.py:17
  266.1 10.1 %collective-permute-start.15 = (f32[1,256,256]{2,1,0:T(8,128)S(1)}, f32[1,256,256]{2,1,0:T(8,128)S(1)}, u32[]{:S(2)}, u32[]{:S(2)}) collective-permute-start(f32[1,256,256]{2,1,0:T(8,128)S(1)} %get-tuple-element.6), channel_id=1, source_target_pairs={{8,0},{16,8},{24,16},{9,1},{17,9},{25,17},{10,2},{18,10},{26,18},{... | collective-permute-start | bytes 786440 | tf_op jit(solution)/shard_map/ppermute | solution.py:18
  267.4 10.1 %collective-permute-start.14 = (f32[1,256,256]{2,1,0:T(8,128)S(1)}, f32[1,256,256]{2,1,0:T(8,128)S(1)}, u32[]{:S(2)}, u32[]{:S(2)}) collective-permute-start(f32[1,256,256]{2,1,0:T(8,128)S(1)} %get-tuple-element.7), channel_id=1, source_target_pairs={{0,8},{8,16},{16,24},{1,9},{9,17},{17,25},{2,10},{10,18},{18,26},{... | collective-permute-start | bytes 786440 | tf_op jit(solution)/shard_map/ppermute | solution.py:17
  271.9 9.9 %collective-permute-start.13 = (f32[1,256,256]{2,1,0:T(8,128)S(1)}, f32[1,256,256]{2,1,0:T(8,128)S(1)}, u32[]{:S(2)}, u32[]{:S(2)}) collective-permute-start(f32[1,256,256]{2,1,0:T(8,128)S(1)} %get-tuple-element.8), channel_id=1, source_target_pairs={{1,0},{2,1},{3,2},{4,3},{5,4},{6,5},{7,6},{9,8},{10,9},{11,10},{12... | collective-permute-start | bytes 786440 | tf_op jit(solution)/shard_map/ppermute | solution.py:18
Sparse Core Ops, SparseCore 0:
  81.3 15.7 all-gather.2
  100.4 62.7 reduce-scatter.6
  237.2 14.7 all-gather.4
  255.2 62.7 reduce-scatter.8
where the time goes:
time: 330 us; the launch traced here: 329 us
  waiting for transfers between devices  120 us (36%)
  blocking collectives  68.5 us (21%)
  local copies, waits for them, and re-layouts  54.5 us (17%)
  starting transfers between devices  41.4 us (13%)
  matrix products  19.8 us (6%)
  between operations  13.4 us (4%)
  other arithmetic  10.5 us (3%)
    all_gather x2, blocking collectives, body(): row_block = lax.all_gather(ordered, 'col', axis=0, tiled=True)  68.5 us
    unnamed x6, waiting for transfers between devices  57.4 us
    ppermute x8, starting transfers between devices, extended(): before = lax.ppermute(last, axis, up)  30.8 us
    all_gather x2, waiting for transfers between devices, body(): source = lax.all_gather(row_block, ('grp', 'row'), axis=0, tiled=True)  30.7 us
    scatter x4, local copies, waits for them, and re-layouts, place(): return blank.at[row_order].set(values.reshape(n_unknowns, n_cases))  25.1 us
    ppermute x8, waiting for transfers between devices, extended(): after = lax.ppermute(first, axis, down)  24.3 us
    gather x4, local copies, waits for them, and re-layouts, traces(): own = values[row_order].reshape(4, edge_len, n_cases)  18.7 us
    ppermute x8, starting transfers between devices, extended(): after = lax.ppermute(first, axis, down)  10.5 us
  transfers between devices with their start and end apart: 20, of which 16 were waited for; matrix products, arithmetic and copies ran while one was open for 10% of the time, Pallas kernels for 0%

commit v1 on v0

--- a/solution.py
+++ b/solution.py
@@ -5,6 +5,12 @@
 
 ITERS = 2
 OMEGA = 0.6
+
+
+def joined_along(blocks, dim):
+    blocks = jnp.moveaxis(blocks, 0, dim)
+    dims = blocks.shape
+    return blocks.reshape(*dims[:dim], dims[dim] * dims[dim + 1], *dims[dim + 2 :])
 
 
 def extended(shard, sides, width):
@@ -70,7 +76,19 @@
         ordered = lax.dot_general(
             selector, coarse_res, contract_first, preferred_element_type=jnp.float32
         ).astype(jnp.bfloat16)
-        row_block = lax.all_gather(ordered, "col", axis=0, tiled=True)
+        length_2 = lax.axis_size("col")
+        pairs = [(i_2, (i_2 + 1) % length_2) for i_2 in range(length_2)]
+        back = [(b, a) for a, b in pairs]
+        lower, upper = ([], [])
+        for step in range(length_2 - 1):
+            if step % 2 == 0:
+                lower.append(lax.ppermute(lower[-1] if lower else ordered, "col", pairs))
+            else:
+                upper.append(lax.ppermute(upper[-1] if upper else ordered, "col", back))
+        pieces = jnp.stack([*lower[::-1], ordered, *upper])
+        shift = lax.axis_index("col") - len(lower)
+        pieces = pieces[(jnp.arange(length_2) - shift) % length_2]
+        row_block = joined_along(pieces, 0)
         source = lax.all_gather(row_block, ("grp", "row"), axis=0, tiled=True)
         offset = my_col * block_len
         column_part = lax.dynamic_slice_in_dim(source, offset, block_len, 0)

time: 330 us -> 322 us (0.976)
  blocking collectives: 68.5 us -> 0 us
  starting transfers between devices: 41.4 us -> 74.6 us
  waiting for transfers between devices: 120 us -> 145 us
    all_gather x2 -> x0, blocking collectives: 68.5 us -> none  [body(): row_block = lax.all_gather(ordered, 'col', axis=0, tiled=True)]
    ppermute x0 -> x14, starting transfers between devices: none -> 33.2 us  [the longest x6 28.5 us: body(): upper.append(lax.ppermute(upper[-1] if upper else ordered, 'col', back))]
    ppermute x0 -> x14, waiting for transfers between devices: none -> 20.6 us  [the longest x8 20.6 us: body(): lower.append(lax.ppermute(lower[-1] if lower else ordered, 'col', pairs))]
    all_gather x2, waiting for transfers between devices: 30.7 us -> 34.6 us  [body(): source = lax.all_gather(row_block, ('grp', 'row'), axis=0, tiled=True)]
  transfers between devices with their start and end apart: 20 -> 34, of which waited for: 16 -> 24; matrix products, arithmetic and copies ran while one was open for 10% -> 10% of each run, Pallas kernels for 0% -> 0%
where the time goes in v1:
time: 322 us; the launch traced here: 320 us
  waiting for transfers between devices  145 us (45%)
  starting transfers between devices  74.6 us (23%)
  local copies, waits for them, and re-layouts  57.1 us (18%)
  matrix products  19.7 us (6%)
  between operations  13.6 us (4%)
  other arithmetic  10.6 us (3%)
    unnamed x6, waiting for transfers between devices  57.4 us
    all_gather x2, waiting for transfers between devices, body(): source = lax.all_gather(row_block, ('grp', 'row'), axis=0, tiled=True)  34.6 us
    ppermute x8, starting transfers between devices, extended(): before = lax.ppermute(last, axis, up)  30.8 us
    ppermute x6, starting transfers between devices, body(): upper.append(lax.ppermute(upper[-1] if upper else ordered, 'col', back))  28.5 us
    scatter x4, local copies, waits for them, and re-layouts, place(): return blank.at[row_order].set(values.reshape(n_unknowns, n_cases))  25.1 us
    ppermute x8, waiting for transfers between devices, extended(): after = lax.ppermute(first, axis, down)  24.4 us
    ppermute x8, waiting for transfers between devices, body(): lower.append(lax.ppermute(lower[-1] if lower else ordered, 'col', pairs))  20.6 us
    gather x4, local copies, waits for them, and re-layouts, traces(): own = values[row_order].reshape(4, edge_len, n_cases)  18.7 us
  transfers between devices with their start and end apart: 34, of which 24 were waited for; matrix products, arithmetic and copies ran while one was open for 10% of the time, Pallas kernels for 0%

profile of v1, /device:TPU:0, one launch (start us, length us, event | category | flops | bytes accessed | tf_op | source)
XLA Modules:
  0.0 320.5 jit_solution(5504414193921873513)
XLA Ops:
  8.1 1.9 fusion.6
  10.1 4.7 %gather_fusion = f32[1024,256]{1,0:T(8,128)} fusion(f32[1024,256]{1,0:T(8,128)S(1)} %fusion.6, s32[1024]{0:T(1024)S(1)} %broadcast_clamp_fusion), kind=kCustom, calls=%fused_computation | custom fusion | bytes 2101248 | tf_op jit(solution)/shard_map/gather | solution.py:57
  16.0 4.9 %collective-permute-start = (f32[1,256,256]{2,1,0:T(8,128)S(1)}, f32[1,256,256]{2,1,0:T(8,128)S(1)}, u32[]{:S(2)}, u32[]{:S(2)}) collective-permute-start(f32[1,256,256]{2,1,0:T(8,128)S(1)} %get-tuple-element.17), channel_id=1, source_target_pairs={{0,1},{1,2},{2,3},{3,4},{4,5},{5,6},{6,7},{8,9},{9,10},{10,11},{11... | collective-permute-start | bytes 786440 | tf_op jit(solution)/shard_map/ppermute | solution.py:23
  20.9 3.4 %collective-permute-start.2 = (f32[1,256,256]{2,1,0:T(8,128)S(1)}, f32[1,256,256]{2,1,0:T(8,128)S(1)}, u32[]{:S(2)}, u32[]{:S(2)}) collective-permute-start(f32[1,256,256]{2,1,0:T(8,128)S(1)} %get-tuple-element.18), channel_id=1, source_target_pairs={{0,8},{8,16},{16,24},{1,9},{9,17},{17,25},{2,10},{10,18},{18,26},{... | collective-permute-start | bytes 786440 | tf_op jit(solution)/shard_map/ppermute | solution.py:23
  24.4 1.3 collective-permute-start.1
  27.0 4.0 %collective-permute-done.2 = f32[1,256,256]{2,1,0:T(8,128)S(1)} collective-permute-done((f32[1,256,256]{2,1,0:T(8,128)S(1)}, f32[1,256,256]{2,1,0:T(8,128)S(1)}, u32[]{:S(2)}, u32[]{:S(2)}) %collective-permute-start.2) | collective-permute-done | bytes 262176 | tf_op jit(solution)/shard_map/ppermute | solution.py:23
  31.0 2.7 collective-permute-done.1
  33.8 1.3 collective-permute-done.3
  36.1 6.3 %scatter_custom_fusion = f32[1024,256]{1,0:T(8,128)} fusion(s32[1024]{0:T(1024)S(1)} %bitcast.183, f32[1024,256]{1,0:T(8,128)} %bitcast.178, f32[]{:T(128)} %constant.17.clone.1), kind=kCustom, calls=%fused_computation.60 | custom fusion | bytes 1049088 | tf_op jit(solution)/shard_map/scatter | solution.py:54
  42.4 2.5 fusion.27
  44.9 1.4 convolution_convert_fusion.5
  46.3 2.4 collective-permute-start.8
  48.7 4.9 %collective-permute-done.8 = bf16[64,256]{1,0:T(8,128)(2,1)S(1)} collective-permute-done((bf16[64,256]{1,0:T(8,128)(2,1)S(1)}, bf16[64,256]{1,0:T(8,128)(2,1)S(1)}, u32[]{:S(2)}, u32[]{:S(2)}) %collective-permute-start.8) | collective-permute-done | bytes 32800 | tf_op jit(solution)/shard_map/ppermute | solution.py:85
  53.6 4.7 %collective-permute-start.12 = (bf16[64,256]{1,0:T(8,128)(2,1)S(1)}, bf16[64,256]{1,0:T(8,128)(2,1)S(1)}, u32[]{:S(2)}, u32[]{:S(2)}) collective-permute-start(bf16[64,256]{1,0:T(8,128)(2,1)S(1)} %convolution_convert_fusion.5), channel_id=1, source_target_pairs={{1,0},{2,1},{3,2},{4,3},{5,4},{6,5},{7,6},{0,7},{9,8},{10,9},{11,1... | collective-permute-start | bytes 98312 | tf_op jit(solution)/shard_map/ppermute | solution.py:87
  58.3 1.9 collective-permute-done.9
  60.2 4.8 %collective-permute-start.13 = (bf16[64,256]{1,0:T(8,128)(2,1)S(1)}, bf16[64,256]{1,0:T(8,128)(2,1)S(1)}, u32[]{:S(2)}, u32[]{:S(2)}) collective-permute-start(bf16[64,256]{1,0:T(8,128)(2,1)S(1)} %collective-permute-done.12), channel_id=1, source_target_pairs={{1,0},{2,1},{3,2},{4,3},{5,4},{6,5},{7,6},{0,7},{9,8},{10,9},{11,1... | collective-permute-start | bytes 98312 | tf_op jit(solution)/shard_map/ppermute | solution.py:87
  65.0 1.8 collective-permute-done.10
  66.9 4.9 %collective-permute-start.14 = (bf16[64,256]{1,0:T(8,128)(2,1)S(1)}, bf16[64,256]{1,0:T(8,128)(2,1)S(1)}, u32[]{:S(2)}, u32[]{:S(2)}) collective-permute-start(bf16[64,256]{1,0:T(8,128)(2,1)S(1)} %collective-permute-done.13), channel_id=1, source_target_pairs={{1,0},{2,1},{3,2},{4,3},{5,4},{6,5},{7,6},{0,7},{9,8},{10,9},{11,1... | collective-permute-start | bytes 98312 | tf_op jit(solution)/shard_map/ppermute | solution.py:87
  71.7 1.7 collective-permute-done.11
  74.9 17.4 %all-gather.3.cloned.1.call-done = bf16[2048,256]{1,0:T(8,128)(2,1)} async-done(((bf16[512,256]{1,0:T(8,128)(2,1)}), bf16[2048,256]{1,0:T(8,128)(2,1)}) %all-gather.3.cloned.1.call-update) | async-done | bytes 1048592 | tf_op jit(solution)/shard_map/all_gather | solution.py:92
  94.5 2.4 fusion.14
  96.9 4.7 %gather_fusion.1 = f32[1024,256]{1,0:T(8,128)} fusion(f32[1024,256]{1,0:T(8,128)S(1)} %fusion.14, s32[1024]{0:T(1024)S(1)} %broadcast_clamp_fusion), kind=kCustom, calls=%fused_computation.1 | custom fusion | bytes 2101248 | tf_op jit(solution)/shard_map/gather | solution.py:57
  101.6 1.4 slice_bitcast_fusion.11
  102.9 3.4 %collective-permute-start.4 = (f32[1,256,256]{2,1,0:T(8,128)S(1)}, f32[1,256,256]{2,1,0:T(8,128)S(1)}, u32[]{:S(2)}, u32[]{:S(2)}) collective-permute-start(f32[1,256,256]{2,1,0:T(8,128)S(1)} %get-tuple-element.13), channel_id=1, source_target_pairs={{0,1},{1,2},{2,3},{3,4},{4,5},{5,6},{6,7},{8,9},{9,10},{10,11},{11... | collective-permute-start | bytes 786440 | tf_op jit(solution)/shard_map/ppermute | solution.py:23
  107.6 4.6 %collective-permute-start.6 = (f32[1,256,256]{2,1,0:T(8,128)S(1)}, f32[1,256,256]{2,1,0:T(8,128)S(1)}, u32[]{:S(2)}, u32[]{:S(2)}) collective-permute-start(f32[1,256,256]{2,1,0:T(8,128)S(1)} %get-tuple-element.15), channel_id=1, source_target_pairs={{0,8},{8,16},{16,24},{1,9},{9,17},{17,25},{2,10},{10,18},{18,26},{... | collective-permute-start | bytes 786440 | tf_op jit(solution)/shard_map/ppermute | solution.py:23
  113.7 2.7 collective-permute-done.7
  116.4 1.3 collective-permute-done.6
  117.7 4.4 %collective-permute-done.5 = f32[1,256,256]{2,1,0:T(8,128)S(1)} collective-permute-done((f32[1,256,256]{2,1,0:T(8,128)S(1)}, f32[1,256,256]{2,1,0:T(8,128)S(1)}, u32[]{:S(2)}, u32[]{:S(2)}) %collective-permute-start.5) | collective-permute-done | bytes 262176 | tf_op jit(solution)/shard_map/ppermute | solution.py:24
  123.4 6.3 %scatter_custom_fusion.1 = f32[1024,256]{1,0:T(8,128)} fusion(s32[1024]{0:T(1024)S(1)} %bitcast.184, f32[1024,256]{1,0:T(8,128)} %fusion.25, f32[]{:T(128)} %constant.17.clone.1), kind=kCustom, calls=%fused_computation.58 | custom fusion | bytes 1049088 | tf_op jit(solution)/shard_map/scatter | solution.py:54
  129.6 28.8 %reduce-scatter.7.cloned.1.call-done = f32[64,256]{1,0:T(8,128)} async-done(((f32[512,256]{1,0:T(8,128)}), f32[64,256]{1,0:T(8,128)}) %reduce-scatter.7.cloned.1.call-update) | async-done | bytes 65552
  158.4 1.6 copy.30
  160.0 3.0 fusion.21
  163.0 1.9 fusion.8
  164.9 4.7 %gather_fusion.3 = f32[1024,256]{1,0:T(8,128)} fusion(f32[1024,256]{1,0:T(8,128)S(1)} %fusion.8, s32[1024]{0:T(1024)S(1)} %broadcast_clamp_fusion), kind=kCustom, calls=%fused_computation.3 | custom fusion | bytes 2101248 | tf_op jit(solution)/shard_map/gather | solution.py:57
  170.9 3.2 collective-permute-start.15
  174.1 3.4 %collective-permute-start.17 = (f32[1,256,256]{2,1,0:T(8,128)S(1)}, f32[1,256,256]{2,1,0:T(8,128)S(1)}, u32[]{:S(2)}, u32[]{:S(2)}) collective-permute-start(f32[1,256,256]{2,1,0:T(8,128)S(1)} %get-tuple-element.10), channel_id=1, source_target_pairs={{0,8},{8,16},{16,24},{1,9},{9,17},{17,25},{2,10},{10,18},{18,26},{... | collective-permute-start | bytes 786440 | tf_op jit(solution)/shard_map/ppermute | solution.py:23
  177.5 1.3 collective-permute-start.16
  178.8 1.5 collective-permute-start.18
  181.5 4.3 %collective-permute-done.16 = f32[1,256,256]{2,1,0:T(8,128)S(1)} collective-permute-done((f32[1,256,256]{2,1,0:T(8,128)S(1)}, f32[1,256,256]{2,1,0:T(8,128)S(1)}, u32[]{:S(2)}, u32[]{:S(2)}) %collective-permute-start.16) | collective-permute-done | bytes 262176 | tf_op jit(solution)/shard_map/ppermute | solution.py:24
  185.7 1.7 collective-permute-done.18
  188.5 6.3 %scatter_custom_fusion.2 = f32[1024,256]{1,0:T(8,128)} fusion(s32[1024]{0:T(1024)S(1)} %bitcast.185, f32[1024,256]{1,0:T(8,128)} %bitcast.179, f32[]{:T(128)} %constant.17.clone.1), kind=kCustom, calls=%fused_computation.56 | custom fusion | bytes 1049088 | tf_op jit(solution)/shard_map/scatter | solution.py:54
  194.7 2.5 fusion.29
  197.2 1.4 convolution_convert_fusion.3
  198.6 2.3 collective-permute-start.23
  200.9 4.4 %collective-permute-done.23 = bf16[64,256]{1,0:T(8,128)(2,1)S(1)} collective-permute-done((bf16[64,256]{1,0:T(8,128)(2,1)S(1)}, bf16[64,256]{1,0:T(8,128)(2,1)S(1)}, u32[]{:S(2)}, u32[]{:S(2)}) %collective-permute-start.23) | collective-permute-done | bytes 32800 | tf_op jit(solution)/shard_map/ppermute | solution.py:85
  205.3 4.7 %collective-permute-start.27 = (bf16[64,256]{1,0:T(8,128)(2,1)S(1)}, bf16[64,256]{1,0:T(8,128)(2,1)S(1)}, u32[]{:S(2)}, u32[]{:S(2)}) collective-permute-start(bf16[64,256]{1,0:T(8,128)(2,1)S(1)} %convolution_convert_fusion.3), channel_id=1, source_target_pairs={{1,0},{2,1},{3,2},{4,3},{5,4},{6,5},{7,6},{0,7},{9,8},{10,9},{11,1... | collective-permute-start | bytes 98312 | tf_op jit(solution)/shard_map/ppermute | solution.py:87
  210.0 1.9 collective-permute-done.24
  211.9 4.7 %collective-permute-start.28 = (bf16[64,256]{1,0:T(8,128)(2,1)S(1)}, bf16[64,256]{1,0:T(8,128)(2,1)S(1)}, u32[]{:S(2)}, u32[]{:S(2)}) collective-permute-start(bf16[64,256]{1,0:T(8,128)(2,1)S(1)} %collective-permute-done.27), channel_id=1, source_target_pairs={{1,0},{2,1},{3,2},{4,3},{5,4},{6,5},{7,6},{0,7},{9,8},{10,9},{11,1... | collective-permute-start | bytes 98312 | tf_op jit(solution)/shard_map/ppermute | solution.py:87
  216.6 2.0 collective-permute-done.25
  218.7 4.7 %collective-permute-start.29 = (bf16[64,256]{1,0:T(8,128)(2,1)S(1)}, bf16[64,256]{1,0:T(8,128)(2,1)S(1)}, u32[]{:S(2)}, u32[]{:S(2)}) collective-permute-start(bf16[64,256]{1,0:T(8,128)(2,1)S(1)} %collective-permute-done.28), channel_id=1, source_target_pairs={{1,0},{2,1},{3,2},{4,3},{5,4},{6,5},{7,6},{0,7},{9,8},{10,9},{11,1... | collective-permute-start | bytes 98312 | tf_op jit(solution)/shard_map/ppermute | solution.py:87
  223.4 1.9 collective-permute-done.26
  225.4 1.4 gather_fusion.5
  226.8 17.2 %all-gather.5.cloned.1.call-done = bf16[2048,256]{1,0:T(8,128)(2,1)} async-done(((bf16[512,256]{1,0:T(8,128)(2,1)}), bf16[2048,256]{1,0:T(8,128)(2,1)}) %all-gather.5.cloned.1.call-update) | async-done | bytes 1048592 | tf_op jit(solution)/shard_map/all_gather | solution.py:92
  246.2 2.4 fusion.11
  248.6 4.7 %gather_fusion.4 = f32[1024,256]{1,0:T(8,128)} fusion(f32[1024,256]{1,0:T(8,128)S(1)} %fusion.11, s32[1024]{0:T(1024)S(1)} %broadcast_clamp_fusion), kind=kCustom, calls=%fused_computation.4 | custom fusion | bytes 2101248 | tf_op jit(solution)/shard_map/gather | solution.py:57
  253.3 1.4 slice_bitcast_fusion.3
  254.7 3.4 %collective-permute-start.19 = (f32[1,256,256]{2,1,0:T(8,128)S(1)}, f32[1,256,256]{2,1,0:T(8,128)S(1)}, u32[]{:S(2)}, u32[]{:S(2)}) collective-permute-start(f32[1,256,256]{2,1,0:T(8,128)S(1)} %get-tuple-element.5), channel_id=1, source_target_pairs={{0,1},{1,2},{2,3},{3,4},{4,5},{5,6},{6,7},{8,9},{9,10},{10,11},{11... | collective-permute-start | bytes 786440 | tf_op jit(solution)/shard_map/ppermute | solution.py:23
  259.3 4.6 %collective-permute-start.21 = (f32[1,256,256]{2,1,0:T(8,128)S(1)}, f32[1,256,256]{2,1,0:T(8,128)S(1)}, u32[]{:S(2)}, u32[]{:S(2)}) collective-permute-start(f32[1,256,256]{2,1,0:T(8,128)S(1)} %get-tuple-element.7), channel_id=1, source_target_pairs={{0,8},{8,16},{16,24},{1,9},{9,17},{17,25},{2,10},{10,18},{18,26},{... | collective-permute-start | bytes 786440 | tf_op jit(solution)/shard_map/ppermute | solution.py:23
  265.2 2.9 collective-permute-done.22
  268.1 1.3 collective-permute-done.21
  269.4 4.4 %collective-permute-done.20 = f32[1,256,256]{2,1,0:T(8,128)S(1)} collective-permute-done((f32[1,256,256]{2,1,0:T(8,128)S(1)}, f32[1,256,256]{2,1,0:T(8,128)S(1)}, u32[]{:S(2)}, u32[]{:S(2)}) %collective-permute-start.20) | collective-permute-done | bytes 262176 | tf_op jit(solution)/shard_map/ppermute | solution.py:24
  275.1 6.3 %scatter_custom_fusion.3 = f32[1024,256]{1,0:T(8,128)} fusion(s32[1024]{0:T(1024)S(1)} %bitcast.186, f32[1024,256]{1,0:T(8,128)} %fusion.24, f32[]{:T(128)} %constant.17.clone.1), kind=kCustom, calls=%fused_computation.54 | custom fusion | bytes 1049088 | tf_op jit(solution)/shard_map/scatter | solution.py:54
  281.4 28.6 %reduce-scatter.9.cloned.1.call-done = f32[64,256]{1,0:T(8,128)} async-done(((f32[512,256]{1,0:T(8,128)}), f32[64,256]{1,0:T(8,128)}) %reduce-scatter.9.cloned.1.call-update) | async-done | bytes 65552
  310.9 3.0 fusion.23
  (81 shorter events, 23.4 us)
Async XLA Ops:
  6.5 1.6 copy-start
  6.5 85.7 %all-gather.3.cloned.1.call-start = ((), (), s32[]{:S(2)}) async-start(), calls=%async_computation.2 | async-start | bytes 1310720 | tf_op jit(solution)/shard_map/all_gather | solution.py:92
  16.0 10.9 %collective-permute-start = (f32[1,256,256]{2,1,0:T(8,128)S(1)}, f32[1,256,256]{2,1,0:T(8,128)S(1)}, u32[]{:S(2)}, u32[]{:S(2)}) collective-permute-start(f32[1,256,256]{2,1,0:T(8,128)S(1)} %get-tuple-element.17), channel_id=1, source_target_pairs={{0,1},{1,2},{2,3},{3,4},{4,5},{5,6},{6,7},{8,9},{9,10},{10,11},{11... | collective-permute-start | bytes 786440 | tf_op jit(solution)/shard_map/ppermute | solution.py:23
  20.9 10.1 %collective-permute-start.2 = (f32[1,256,256]{2,1,0:T(8,128)S(1)}, f32[1,256,256]{2,1,0:T(8,128)S(1)}, u32[]{:S(2)}, u32[]{:S(2)}) collective-permute-start(f32[1,256,256]{2,1,0:T(8,128)S(1)} %get-tuple-element.18), channel_id=1, source_target_pairs={{0,8},{8,16},{16,24},{1,9},{9,17},{17,25},{2,10},{10,18},{18,26},{... | collective-permute-start | bytes 786440 | tf_op jit(solution)/shard_map/ppermute | solution.py:23
  24.4 9.4 %collective-permute-start.1 = (f32[1,256,256]{2,1,0:T(8,128)S(1)}, f32[1,256,256]{2,1,0:T(8,128)S(1)}, u32[]{:S(2)}, u32[]{:S(2)}) collective-permute-start(f32[1,256,256]{2,1,0:T(8,128)S(1)} %get-tuple-element.19), channel_id=1, source_target_pairs={{1,0},{2,1},{3,2},{4,3},{5,4},{6,5},{7,6},{9,8},{10,9},{11,10},{12... | collective-permute-start | bytes 786440 | tf_op jit(solution)/shard_map/ppermute | solution.py:24
  25.7 9.4 %collective-permute-start.3 = (f32[1,256,256]{2,1,0:T(8,128)S(1)}, f32[1,256,256]{2,1,0:T(8,128)S(1)}, u32[]{:S(2)}, u32[]{:S(2)}) collective-permute-start(f32[1,256,256]{2,1,0:T(8,128)S(1)} %get-tuple-element.20), channel_id=1, source_target_pairs={{8,0},{16,8},{24,16},{9,1},{17,9},{25,17},{10,2},{18,10},{26,18},{... | collective-permute-start | bytes 786440 | tf_op jit(solution)/shard_map/ppermute | solution.py:24
  42.4 2.6 copy-start.3
  42.4 2.6 copy-start.5
  42.4 49.9 %copy-start.4 = (bf16[512,256]{1,0:T(8,128)(2,1)S(1)}, bf16[512,256]{1,0:T(8,128)(2,1)}, u32[]{:S(2)}) copy-start(bf16[512,256]{1,0:T(8,128)(2,1)} %param.13) | copy-start | bytes 786436
  46.3 7.3 %collective-permute-start.8 = (bf16[64,256]{1,0:T(8,128)(2,1)S(1)}, bf16[64,256]{1,0:T(8,128)(2,1)S(1)}, u32[]{:S(2)}, u32[]{:S(2)}) collective-permute-start(bf16[64,256]{1,0:T(8,128)(2,1)S(1)} %convolution_convert_fusion.5), channel_id=1, source_target_pairs={{0,1},{1,2},{2,3},{3,4},{4,5},{5,6},{6,7},{7,0},{8,9},{9,10},{10,1... | collective-permute-start | bytes 98312 | tf_op jit(solution)/shard_map/ppermute | solution.py:85
  53.6 6.6 %collective-permute-start.9 = (bf16[64,256]{1,0:T(8,128)(2,1)S(1)}, bf16[64,256]{1,0:T(8,128)(2,1)S(1)}, u32[]{:S(2)}, u32[]{:S(2)}) collective-permute-start(bf16[64,256]{1,0:T(8,128)(2,1)S(1)} %collective-permute-done.8), channel_id=1, source_target_pairs={{0,1},{1,2},{2,3},{3,4},{4,5},{5,6},{6,7},{7,0},{8,9},{9,10},{10,1... | collective-permute-start | bytes 98312 | tf_op jit(solution)/shard_map/ppermute | solution.py:85
  53.6 6.6 %collective-permute-start.12 = (bf16[64,256]{1,0:T(8,128)(2,1)S(1)}, bf16[64,256]{1,0:T(8,128)(2,1)S(1)}, u32[]{:S(2)}, u32[]{:S(2)}) collective-permute-start(bf16[64,256]{1,0:T(8,128)(2,1)S(1)} %convolution_convert_fusion.5), channel_id=1, source_target_pairs={{1,0},{2,1},{3,2},{4,3},{5,4},{6,5},{7,6},{0,7},{9,8},{10,9},{11,1... | collective-permute-start | bytes 98312 | tf_op jit(solution)/shard_map/ppermute | solution.py:87
  60.2 6.6 %collective-permute-start.10 = (bf16[64,256]{1,0:T(8,128)(2,1)S(1)}, bf16[64,256]{1,0:T(8,128)(2,1)S(1)}, u32[]{:S(2)}, u32[]{:S(2)}) collective-permute-start(bf16[64,256]{1,0:T(8,128)(2,1)S(1)} %collective-permute-done.9), channel_id=1, source_target_pairs={{0,1},{1,2},{2,3},{3,4},{4,5},{5,6},{6,7},{7,0},{8,9},{9,10},{10,1... | collective-permute-start | bytes 98312 | tf_op jit(solution)/shard_map/ppermute | solution.py:85
  60.2 6.6 %collective-permute-start.13 = (bf16[64,256]{1,0:T(8,128)(2,1)S(1)}, bf16[64,256]{1,0:T(8,128)(2,1)S(1)}, u32[]{:S(2)}, u32[]{:S(2)}) collective-permute-start(bf16[64,256]{1,0:T(8,128)(2,1)S(1)} %collective-permute-done.12), channel_id=1, source_target_pairs={{1,0},{2,1},{3,2},{4,3},{5,4},{6,5},{7,6},{0,7},{9,8},{10,9},{11,1... | collective-permute-start | bytes 98312 | tf_op jit(solution)/shard_map/ppermute | solution.py:87
  66.8 6.6 %collective-permute-start.11 = (bf16[64,256]{1,0:T(8,128)(2,1)S(1)}, bf16[64,256]{1,0:T(8,128)(2,1)S(1)}, u32[]{:S(2)}, u32[]{:S(2)}) collective-permute-start(bf16[64,256]{1,0:T(8,128)(2,1)S(1)} %collective-permute-done.10), channel_id=1, source_target_pairs={{0,1},{1,2},{2,3},{3,4},{4,5},{5,6},{6,7},{7,0},{8,9},{9,10},{10,1... | collective-permute-start | bytes 98312 | tf_op jit(solution)/shard_map/ppermute | solution.py:85
  66.8 30.0 %copy-start.6 = (s32[1024]{0:T(1024)}, s32[1024]{0:T(1024)S(1)}, u32[]{:S(2)}) copy-start(s32[1024]{0:T(1024)S(1)} %pad_clamp_fusion) | copy-start | bytes 12292
  66.9 6.6 %collective-permute-start.14 = (bf16[64,256]{1,0:T(8,128)(2,1)S(1)}, bf16[64,256]{1,0:T(8,128)(2,1)S(1)}, u32[]{:S(2)}, u32[]{:S(2)}) collective-permute-start(bf16[64,256]{1,0:T(8,128)(2,1)S(1)} %collective-permute-done.13), channel_id=1, source_target_pairs={{1,0},{2,1},{3,2},{4,3},{5,4},{6,5},{7,6},{0,7},{9,8},{10,9},{11,1... | collective-permute-start | bytes 98312 | tf_op jit(solution)/shard_map/ppermute | solution.py:87
  74.8 83.6 %reduce-scatter.7.cloned.1.call-start = ((), (), s32[]{:S(2)}) async-start(), calls=%async_computation.4 | async-start | bytes 589824
  94.4 149.6 %all-gather.5.cloned.1.call-start = ((), (), s32[]{:S(2)}) async-start(), calls=%async_computation.3 | async-start | bytes 1310720 | tf_op jit(solution)/shard_map/all_gather | solution.py:92
  101.6 20.6 %copy-start.1 = (f32[1024,256]{1,0:T(8,128)S(1)}, f32[1024,256]{1,0:T(8,128)}, u32[]{:S(2)}) copy-start(f32[1024,256]{1,0:T(8,128)} %gather_fusion.1) | copy-start | bytes 3145732
  102.9 10.7 %collective-permute-start.4 = (f32[1,256,256]{2,1,0:T(8,128)S(1)}, f32[1,256,256]{2,1,0:T(8,128)S(1)}, u32[]{:S(2)}, u32[]{:S(2)}) collective-permute-start(f32[1,256,256]{2,1,0:T(8,128)S(1)} %get-tuple-element.13), channel_id=1, source_target_pairs={{0,1},{1,2},{2,3},{3,4},{4,5},{5,6},{6,7},{8,9},{9,10},{10,11},{11... | collective-permute-start | bytes 786440 | tf_op jit(solution)/shard_map/ppermute | solution.py:23
  106.3 10.0 %collective-permute-start.7 = (f32[1,256,256]{2,1,0:T(8,128)S(1)}, f32[1,256,256]{2,1,0:T(8,128)S(1)}, u32[]{:S(2)}, u32[]{:S(2)}) collective-permute-start(f32[1,256,256]{2,1,0:T(8,128)S(1)} %get-tuple-element.14), channel_id=1, source_target_pairs={{8,0},{16,8},{24,16},{9,1},{17,9},{25,17},{10,2},{18,10},{26,18},{... | collective-permute-start | bytes 786440 | tf_op jit(solution)/shard_map/ppermute | solution.py:24
  107.6 10.1 %collective-permute-start.6 = (f32[1,256,256]{2,1,0:T(8,128)S(1)}, f32[1,256,256]{2,1,0:T(8,128)S(1)}, u32[]{:S(2)}, u32[]{:S(2)}) collective-permute-start(f32[1,256,256]{2,1,0:T(8,128)S(1)} %get-tuple-element.15), channel_id=1, source_target_pairs={{0,8},{8,16},{16,24},{1,9},{9,17},{17,25},{2,10},{10,18},{18,26},{... | collective-permute-start | bytes 786440 | tf_op jit(solution)/shard_map/ppermute | solution.py:23
  112.2 9.9 %collective-permute-start.5 = (f32[1,256,256]{2,1,0:T(8,128)S(1)}, f32[1,256,256]{2,1,0:T(8,128)S(1)}, u32[]{:S(2)}, u32[]{:S(2)}) collective-permute-start(f32[1,256,256]{2,1,0:T(8,128)S(1)} %get-tuple-element.16), channel_id=1, source_target_pairs={{1,0},{2,1},{3,2},{4,3},{5,4},{6,5},{7,6},{9,8},{10,9},{11,10},{12... | collective-permute-start | bytes 786440 | tf_op jit(solution)/shard_map/ppermute | solution.py:24
  170.9 9.4 %collective-permute-start.15 = (f32[1,256,256]{2,1,0:T(8,128)S(1)}, f32[1,256,256]{2,1,0:T(8,128)S(1)}, u32[]{:S(2)}, u32[]{:S(2)}) collective-permute-start(f32[1,256,256]{2,1,0:T(8,128)S(1)} %get-tuple-element.9), channel_id=1, source_target_pairs={{0,1},{1,2},{2,3},{3,4},{4,5},{5,6},{6,7},{8,9},{9,10},{10,11},{11... | collective-permute-start | bytes 786440 | tf_op jit(solution)/shard_map/ppermute | solution.py:23
  174.1 7.4 %collective-permute-start.17 = (f32[1,256,256]{2,1,0:T(8,128)S(1)}, f32[1,256,256]{2,1,0:T(8,128)S(1)}, u32[]{:S(2)}, u32[]{:S(2)}) collective-permute-start(f32[1,256,256]{2,1,0:T(8,128)S(1)} %get-tuple-element.10), channel_id=1, source_target_pairs={{0,8},{8,16},{16,24},{1,9},{9,17},{17,25},{2,10},{10,18},{18,26},{... | collective-permute-start | bytes 786440 | tf_op jit(solution)/shard_map/ppermute | solution.py:23
  177.5 8.3 %collective-permute-start.16 = (f32[1,256,256]{2,1,0:T(8,128)S(1)}, f32[1,256,256]{2,1,0:T(8,128)S(1)}, u32[]{:S(2)}, u32[]{:S(2)}) collective-permute-start(f32[1,256,256]{2,1,0:T(8,128)S(1)} %get-tuple-element.11), channel_id=1, source_target_pairs={{1,0},{2,1},{3,2},{4,3},{5,4},{6,5},{7,6},{9,8},{10,9},{11,10},{12... | collective-permute-start | bytes 786440 | tf_op jit(solution)/shard_map/ppermute | solution.py:24
  178.8 8.6 %collective-permute-start.18 = (f32[1,256,256]{2,1,0:T(8,128)S(1)}, f32[1,256,256]{2,1,0:T(8,128)S(1)}, u32[]{:S(2)}, u32[]{:S(2)}) collective-permute-start(f32[1,256,256]{2,1,0:T(8,128)S(1)} %get-tuple-element.12), channel_id=1, source_target_pairs={{8,0},{16,8},{24,16},{9,1},{17,9},{25,17},{10,2},{18,10},{26,18},{... | collective-permute-start | bytes 786440 | tf_op jit(solution)/shard_map/ppermute | solution.py:24
  198.6 6.7 %collective-permute-start.23 = (bf16[64,256]{1,0:T(8,128)(2,1)S(1)}, bf16[64,256]{1,0:T(8,128)(2,1)S(1)}, u32[]{:S(2)}, u32[]{:S(2)}) collective-permute-start(bf16[64,256]{1,0:T(8,128)(2,1)S(1)} %convolution_convert_fusion.3), channel_id=1, source_target_pairs={{0,1},{1,2},{2,3},{3,4},{4,5},{5,6},{6,7},{7,0},{8,9},{9,10},{10,1... | collective-permute-start | bytes 98312 | tf_op jit(solution)/shard_map/ppermute | solution.py:85
  205.3 6.6 %collective-permute-start.24 = (bf16[64,256]{1,0:T(8,128)(2,1)S(1)}, bf16[64,256]{1,0:T(8,128)(2,1)S(1)}, u32[]{:S(2)}, u32[]{:S(2)}) collective-permute-start(bf16[64,256]{1,0:T(8,128)(2,1)S(1)} %collective-permute-done.23), channel_id=1, source_target_pairs={{0,1},{1,2},{2,3},{3,4},{4,5},{5,6},{6,7},{7,0},{8,9},{9,10},{10,1... | collective-permute-start | bytes 98312 | tf_op jit(solution)/shard_map/ppermute | solution.py:85
  205.3 6.6 %collective-permute-start.27 = (bf16[64,256]{1,0:T(8,128)(2,1)S(1)}, bf16[64,256]{1,0:T(8,128)(2,1)S(1)}, u32[]{:S(2)}, u32[]{:S(2)}) collective-permute-start(bf16[64,256]{1,0:T(8,128)(2,1)S(1)} %convolution_convert_fusion.3), channel_id=1, source_target_pairs={{1,0},{2,1},{3,2},{4,3},{5,4},{6,5},{7,6},{0,7},{9,8},{10,9},{11,1... | collective-permute-start | bytes 98312 | tf_op jit(solution)/shard_map/ppermute | solution.py:87
  211.9 6.8 %collective-permute-start.25 = (bf16[64,256]{1,0:T(8,128)(2,1)S(1)}, bf16[64,256]{1,0:T(8,128)(2,1)S(1)}, u32[]{:S(2)}, u32[]{:S(2)}) collective-permute-start(bf16[64,256]{1,0:T(8,128)(2,1)S(1)} %collective-permute-done.24), channel_id=1, source_target_pairs={{0,1},{1,2},{2,3},{3,4},{4,5},{5,6},{6,7},{7,0},{8,9},{9,10},{10,1... | collective-permute-start | bytes 98312 | tf_op jit(solution)/shard_map/ppermute | solution.py:85
  211.9 6.8 %collective-permute-start.28 = (bf16[64,256]{1,0:T(8,128)(2,1)S(1)}, bf16[64,256]{1,0:T(8,128)(2,1)S(1)}, u32[]{:S(2)}, u32[]{:S(2)}) collective-permute-start(bf16[64,256]{1,0:T(8,128)(2,1)S(1)} %collective-permute-done.27), channel_id=1, source_target_pairs={{1,0},{2,1},{3,2},{4,3},{5,4},{6,5},{7,6},{0,7},{9,8},{10,9},{11,1... | collective-permute-start | bytes 98312 | tf_op jit(solution)/shard_map/ppermute | solution.py:87
  218.7 6.6 %collective-permute-start.26 = (bf16[64,256]{1,0:T(8,128)(2,1)S(1)}, bf16[64,256]{1,0:T(8,128)(2,1)S(1)}, u32[]{:S(2)}, u32[]{:S(2)}) collective-permute-start(bf16[64,256]{1,0:T(8,128)(2,1)S(1)} %collective-permute-done.25), channel_id=1, source_target_pairs={{0,1},{1,2},{2,3},{3,4},{4,5},{5,6},{6,7},{7,0},{8,9},{9,10},{10,1... | collective-permute-start | bytes 98312 | tf_op jit(solution)/shard_map/ppermute | solution.py:85
  218.7 6.7 %collective-permute-start.29 = (bf16[64,256]{1,0:T(8,128)(2,1)S(1)}, bf16[64,256]{1,0:T(8,128)(2,1)S(1)}, u32[]{:S(2)}, u32[]{:S(2)}) collective-permute-start(bf16[64,256]{1,0:T(8,128)(2,1)S(1)} %collective-permute-done.28), channel_id=1, source_target_pairs={{1,0},{2,1},{3,2},{4,3},{5,4},{6,5},{7,6},{0,7},{9,8},{10,9},{11,1... | collective-permute-start | bytes 98312 | tf_op jit(solution)/shard_map/ppermute | solution.py:87
  226.8 83.2 %reduce-scatter.9.cloned.1.call-start = ((), (), s32[]{:S(2)}) async-start(), calls=%async_computation.5 | async-start | bytes 589824
  253.3 20.6 %copy-start.2 = (f32[1024,256]{1,0:T(8,128)S(1)}, f32[1024,256]{1,0:T(8,128)}, u32[]{:S(2)}) copy-start(f32[1024,256]{1,0:T(8,128)} %gather_fusion.4) | copy-start | bytes 3145732
  254.7 10.5 %collective-permute-start.19 = (f32[1,256,256]{2,1,0:T(8,128)S(1)}, f32[1,256,256]{2,1,0:T(8,128)S(1)}, u32[]{:S(2)}, u32[]{:S(2)}) collective-permute-start(f32[1,256,256]{2,1,0:T(8,128)S(1)} %get-tuple-element.5), channel_id=1, source_target_pairs={{0,1},{1,2},{2,3},{3,4},{4,5},{5,6},{6,7},{8,9},{9,10},{10,11},{11... | collective-permute-start | bytes 786440 | tf_op jit(solution)/shard_map/ppermute | solution.py:23
  258.0 10.1 %collective-permute-start.22 = (f32[1,256,256]{2,1,0:T(8,128)S(1)}, f32[1,256,256]{2,1,0:T(8,128)S(1)}, u32[]{:S(2)}, u32[]{:S(2)}) collective-permute-start(f32[1,256,256]{2,1,0:T(8,128)S(1)} %get-tuple-element.6), channel_id=1, source_target_pairs={{8,0},{16,8},{24,16},{9,1},{17,9},{25,17},{10,2},{18,10},{26,18},{... | collective-permute-start | bytes 786440 | tf_op jit(solution)/shard_map/ppermute | solution.py:24
  259.3 10.1 %collective-permute-start.21 = (f32[1,256,256]{2,1,0:T(8,128)S(1)}, f32[1,256,256]{2,1,0:T(8,128)S(1)}, u32[]{:S(2)}, u32[]{:S(2)}) collective-permute-start(f32[1,256,256]{2,1,0:T(8,128)S(1)} %get-tuple-element.7), channel_id=1, source_target_pairs={{0,8},{8,16},{16,24},{1,9},{9,17},{17,25},{2,10},{10,18},{18,26},{... | collective-permute-start | bytes 786440 | tf_op jit(solution)/shard_map/ppermute | solution.py:23
  263.9 9.9 %collective-permute-start.20 = (f32[1,256,256]{2,1,0:T(8,128)S(1)}, f32[1,256,256]{2,1,0:T(8,128)S(1)}, u32[]{:S(2)}, u32[]{:S(2)}) collective-permute-start(f32[1,256,256]{2,1,0:T(8,128)S(1)} %get-tuple-element.8), channel_id=1, source_target_pairs={{1,0},{2,1},{3,2},{4,3},{5,4},{6,5},{7,6},{9,8},{10,9},{11,10},{12... | collective-permute-start | bytes 786440 | tf_op jit(solution)/shard_map/ppermute | solution.py:24
Sparse Core Ops, SparseCore 0:
  74.9 17.2 all-gather.2
  95.6 62.8 reduce-scatter.6
  226.9 17.0 all-gather.4
  247.2 62.7 reduce-scatter.8
